TPU v7x, 256 devices: a whole 4x4x8 slice. The times are simulated.
256 devices in a mesh: view: 2 (over x_hi), seq: 8 (over y, core), event: 16 (over x_lo, z).
Axes of the slice: x: 4 (x_hi: 2, x_lo: 2; x = x_hi * 2 + x_lo), y: 4, z: 8, core: 2. Of those that a mesh axis runs over, the one named last changes fastest.
Arguments:
- query: bfloat16 [16, 2, 3072, 512], P('event', 'view', 'seq'), may hold values from -7 to 7
- key: bfloat16 [16, 2, 3072, 512], P('event', 'view', 'seq'), may hold values from -7 to 7
- value: bfloat16 [16, 2, 3072, 512], P('event', 'view', 'seq'), may hold values from -6 to 6
- pattern: int32 [16, 2, 24, 24], P('event', 'view', 'seq'), may hold values from 0 to 1, as said below
- out_weight: bfloat16 [512, 512], replicated, may hold values from -0.25 to 0.25
- served: int32 [16, 2, 128, 128], P('event', 'view', 'seq'), may hold values from 0 to 383
- anchor_rows: int32 [16, 2, 2048], P('event', 'view', 'seq'), may hold values from 0 to 383
- positive_slot: int32 [16, 2, 2048], P('event', 'view', 'seq'), may hold values from 0 to 2047, as said below
- anchor_live: int32 [16, 2, 2048], P('event', 'view', 'seq'), may hold values from 0 to 1, as said below
Outputs:
- mixed: bfloat16 [16, 2, 3072, 512], P('event', 'view', 'seq')
- grad_wo: float32 [512, 512], replicated
- loss: float32 [], replicated
Inputs may be any that keep to these rules, and one draw needn't show every extreme that they name: pattern[e, v, b, b] is 1 for every block b. `positive_slot`: for an anchor of view v the slot lies in [(1 - v) * 1024, (2 - v) * 1024), a point of the other view. `anchor_live`: every device's block of 256 anchors holds at least one live anchor.
All inputs are finite; a program needn't handle non-finite values.
Results may differ from a plain program's by a relative error of at most 0.015.
Values may be sent and summed in bfloat16 or wider, within the bound.
No kernel may reach another device: no remote copies, remote signals or barrier semaphores. Data moves between devices by JAX's collectives and lax.ppermute only.
A program may use at most 64 MiB of HBM per device.

v0:
```python
import jax
import jax.numpy as jnp
from jax import lax
from jax.sharding import PartitionSpec as P

HEADS = 16
BLOCK = 128
NEGATIVE = -1e30
SHARPNESS_SCALE = 0.07


def from_behind(array, axis, by):
    peers = lax.axis_size(axis)
    return lax.ppermute(array, axis, [(i, (i + by) % peers) for i in range(peers)])


def per_device(
    query, key, value, pattern, out_weight, served, anchor_rows, positive_slot, anchor_live
):
    queries = query[0, 0]
    keys = key[0, 0]
    values = value[0, 0]
    points, width = queries.shape
    head_dim = width // HEADS
    scale = head_dim ** (-0.5)
    loop_size = lax.axis_size("seq")
    myself = lax.axis_index("seq")
    local_pattern = pattern[0, 0].astype(jnp.float32)
    blocks_dev, blocks_all = local_pattern.shape
    query_block = jnp.arange(points) // BLOCK
    pick_rows = (query_block[:, None] == jnp.arange(blocks_dev)[None, :]).astype(jnp.float32)
    row_pattern = jnp.dot(pick_rows, local_pattern, preferred_element_type=jnp.float32)
    head_queries = queries.reshape(points, HEADS, head_dim)

    def attend(state, key_piece, value_piece, start):
        length = key_piece.shape[0]
        count = length // BLOCK
        size = BLOCK
        key_groups = key_piece.reshape(count, size, width)
        value_groups = value_piece.reshape(count, size, width)
        offsets = start + jnp.arange(count, dtype=jnp.int32) * size

        def one_group(carry, inputs):
            key_group, value_group, offset = inputs
            key_block = (offset + jnp.arange(size)) // BLOCK
            pick_keys = (jnp.arange(blocks_all)[:, None] == key_block[None, :]).astype(jnp.float32)
            allowed = jnp.dot(row_pattern, pick_keys, preferred_element_type=jnp.float32) > 0.5
            best, total, accum = carry
            head_keys = key_group.reshape(size, HEADS, head_dim)
            head_values = value_group.reshape(size, HEADS, head_dim)
            scores = (
                jnp.einsum(
                    "qhd,khd->hqk", head_queries, head_keys, preferred_element_type=jnp.float32
                )
                * scale
            )
            scores = jnp.where(allowed[None], scores, NEGATIVE)
            new_best = jnp.maximum(best, jnp.max(scores, axis=-1))
            weights = jnp.where(allowed[None], jnp.exp(scores - new_best[..., None]), 0.0)
            factor = jnp.exp(best - new_best)
            total = total * factor + jnp.sum(weights, axis=-1)
            added = jnp.einsum(
                "hqk,khd->hqd",
                weights.astype(jnp.bfloat16),
                head_values,
                preferred_element_type=jnp.float32,
            )
            result = (new_best, total, accum * factor[..., None] + added)
            return (result, None)

        final_state, unused = lax.scan(one_group, state, (key_groups, value_groups, offsets))
        return final_state

    initial = (
        jnp.full((HEADS, points), NEGATIVE, jnp.float32),
        jnp.zeros((HEADS, points), jnp.float32),
        jnp.zeros((HEADS, points, head_dim), jnp.float32),
    )
    state = attend(initial, keys, values, myself * points)
    moving = (keys, values)
    for step in range(1, loop_size):
        moving = from_behind((moving[0], moving[1]), "seq", 1)
        root = (myself - step) % loop_size
        state = attend(state, moving[0], moving[1], root * points)
    best, total, accum = state
    mixed = (
        (accum / total[..., None]).transpose(1, 0, 2).reshape(points, width).astype(jnp.bfloat16)
    )
    embedding_rows = jnp.dot(mixed, out_weight, preferred_element_type=jnp.float32)
    inverse = lax.rsqrt(jnp.sum(embedding_rows * embedding_rows, axis=-1) + 1e-06)
    unit = (embedding_rows * inverse[:, None]).astype(jnp.bfloat16)
    served_rows = served[0, 0]
    senders, capacity = served_rows.shape
    flat_served = served_rows.reshape(-1)
    outgoing = jnp.take(unit, flat_served, axis=0).reshape(senders, capacity, width)
    incoming = lax.all_to_all(outgoing, ("view", "seq"), split_axis=0, concat_axis=0, tiled=True)
    contender_vectors = incoming.reshape(senders * capacity, width)
    own_rows = anchor_rows[0, 0]
    query_vectors = jnp.take(unit, own_rows, axis=0)
    pairwise_scores = (
        lax.dot_general(
            query_vectors,
            contender_vectors,
            (((1,), (1,)), ((), ())),
            preferred_element_type=jnp.float32,
        )
        / SHARPNESS_SCALE
    )
    exponentiated_scores = jnp.exp(pairwise_scores)
    partition_totals = jnp.sum(exponentiated_scores, axis=-1)
    log_total = jnp.log(partition_totals)
    correct_column = (
        jnp.arange(senders * capacity)[None, :] == positive_slot[0, 0][:, None]
    ).astype(jnp.float32)
    active_queries = anchor_live[0, 0].astype(jnp.float32)
    loss_part = jnp.sum(
        active_queries * (log_total - jnp.sum(pairwise_scores * correct_column, axis=-1))
    )
    live_part = jnp.sum(active_queries)
    score_derivatives = (
        active_queries[:, None]
        * (exponentiated_scores / partition_totals[:, None] - correct_column)
        / SHARPNESS_SCALE
    )
    anchor_grads = jnp.dot(
        score_derivatives, contender_vectors.astype(jnp.float32), precision=lax.Precision.HIGHEST
    )
    candidate_grads = lax.dot_general(
        score_derivatives,
        query_vectors.astype(jnp.float32),
        (((0,), (0,)), ((), ())),
        precision=lax.Precision.HIGHEST,
    )
    returned = lax.all_to_all(
        candidate_grads.reshape(senders, capacity, width).astype(jnp.bfloat16),
        ("view", "seq"),
        split_axis=0,
        concat_axis=0,
        tiled=True,
    ).astype(jnp.float32)
    unit_grads = (
        jnp.zeros((points, width), jnp.float32).at[flat_served].add(returned.reshape(-1, width))
    )
    unit_grads = unit_grads.at[own_rows].add(anchor_grads)
    inner = jnp.sum(embedding_rows * unit_grads, axis=-1)
    embedding_gradients = (
        inverse[:, None] * (unit_grads - embedding_rows * (inverse * inverse * inner)[:, None])
    ).astype(jnp.bfloat16)
    loss_term = lax.dot_general(
        mixed, embedding_gradients, (((0,), (0,)), ((), ())), preferred_element_type=jnp.float32
    )
    grad_total, loss_total, live_total = lax.psum(
        (loss_term, loss_part, live_part), ("view", "seq", "event")
    )
    return (mixed[None, None], grad_total, loss_total / live_total)


def solution(mesh):
    placed = (
        P("event", "view", "seq", None),
        P("event", "view", "seq", None),
        P("event", "view", "seq", None),
        P("event", "view", "seq", None),
        P(),
        P("event", "view", "seq", None),
        P("event", "view", "seq"),
        P("event", "view", "seq"),
        P("event", "view", "seq"),
    )
    return jax.shard_map(
        per_device,
        mesh=mesh,
        in_specs=placed,
        out_specs=(P("event", "view", "seq", None), P(), P()),
        check_vma=False,
    )
```

profile of v0, /device:TPU:2, one launch (start us, length us, event | category | flops | bytes accessed | tf_op | source)
XLA Modules:
  0.0 610.7 jit_solution(11017529696734789384)
XLA Ops:
  11.1 31.8 %while.136 = (s32[]{:T(128)}, f32[16,384]{1,0:T(8,128)S(1)}, f32[16,384]{1,0:T(8,128)S(1)}, f32[16,384,32]{1,2,0:T(8,128)S(1)}, s32[3]{0:T(128)S(1)}, /*index=5*...) while((s32[]{:T(128)}, f32[16,384]{1,0:T(8,128)S(1)}, ...), condition=%wide.region_3.4_spmd.clone, body=%wide.region_0.3_spmd.clone.sunk | while | flops 113921024 | bytes 13323405 | solution.py:71
  18.8 2.8 fusion.319
  29.4 2.8 fusion.319
  40.0 2.8 fusion.319
  44.8 26.6 %while.129 = (s32[]{:T(128)}, f32[16,384]{1,0:T(8,128)S(1)}, f32[16,384]{1,0:T(8,128)S(1)}, f32[16,384,32]{1,2,0:T(8,128)S(1)}, s32[3]{0:T(128)S(1)}, /*index=5*...) while((s32[]{:T(128)}, f32[16,384]{1,0:T(8,128)S(1)}, ...), condition=%wide.region_7.8_spmd, body=%wide.region_4.7_spmd.sunk | while | flops 113705984 | bytes 25906324 | solution.py:71
  50.8 2.8 fusion.255
  59.7 2.8 fusion.255
  68.6 2.8 fusion.255
  72.8 26.6 %while.130 = (s32[]{:T(128)}, f32[16,384]{1,0:T(8,128)S(1)}, f32[16,384]{1,0:T(8,128)S(1)}, f32[16,384,32]{1,2,0:T(8,128)S(1)}, s32[3]{0:T(128)S(1)}, /*index=5*...) while((s32[]{:T(128)}, f32[16,384]{1,0:T(8,128)S(1)}, ...), condition=%wide.region_11.12_spmd, body=%wide.region_8.11_spmd.sunk | while | flops 113705984 | bytes 25906324 | solution.py:71
  96.6 2.8 fusion.264
  100.0 26.6 %while.131 = (s32[]{:T(128)}, f32[16,384]{1,0:T(8,128)S(1)}, f32[16,384]{1,0:T(8,128)S(1)}, f32[16,384,32]{1,2,0:T(8,128)S(1)}, s32[3]{0:T(128)S(1)}, /*index=5*...) while((s32[]{:T(128)}, f32[16,384]{1,0:T(8,128)S(1)}, ...), condition=%wide.region_15.16_spmd, body=%wide.region_12.15_spmd.sunk | while | flops 113705984 | bytes 25906324 | solution.py:71
  123.8 2.8 fusion.273
  128.1 26.6 %while.132 = (s32[]{:T(128)}, f32[16,384]{1,0:T(8,128)S(1)}, f32[16,384]{1,0:T(8,128)S(1)}, f32[16,384,32]{1,2,0:T(8,128)S(1)}, s32[3]{0:T(128)S(1)}, /*index=5*...) while((s32[]{:T(128)}, f32[16,384]{1,0:T(8,128)S(1)}, ...), condition=%wide.region_19.20_spmd, body=%wide.region_16.19_spmd.sunk | while | flops 113705984 | bytes 25906324 | solution.py:71
  134.2 2.8 fusion.282
  156.5 26.6 %while.133 = (s32[]{:T(128)}, f32[16,384]{1,0:T(8,128)S(1)}, f32[16,384]{1,0:T(8,128)S(1)}, f32[16,384,32]{1,2,0:T(8,128)S(1)}, s32[3]{0:T(128)S(1)}, /*index=5*...) while((s32[]{:T(128)}, f32[16,384]{1,0:T(8,128)S(1)}, ...), condition=%wide.region_23.24_spmd, body=%wide.region_20.23_spmd.sunk | while | flops 113705984 | bytes 25906324 | solution.py:71
  162.5 2.8 fusion.291
  171.4 2.8 fusion.291
  184.5 26.0 %while.134 = (s32[]{:T(128)}, f32[16,384]{1,0:T(8,128)S(1)}, f32[16,384]{1,0:T(8,128)S(1)}, f32[16,384,32]{1,2,0:T(8,128)S(1)}, s32[3]{0:T(128)S(1)}, /*index=5*...) while((s32[]{:T(128)}, f32[16,384]{1,0:T(8,128)S(1)}, ...), condition=%wide.region_27.28_spmd, body=%wide.region_24.27_spmd.sunk | while | flops 113705984 | bytes 25906324 | solution.py:71
  199.0 2.8 fusion.300
  207.7 2.8 fusion.300
  210.5 23.4 %while.135 = (s32[]{:T(128)}, f32[16,384]{1,0:T(8,128)S(1)}, f32[16,384]{1,0:T(8,128)S(1)}, f32[16,384,32]{1,2,0:T(8,128)S(1)}, s32[3]{0:T(128)S(1)}, /*index=5*...) while((s32[]{:T(128)}, f32[16,384]{1,0:T(8,128)S(1)}, ...), condition=%wide.region_31.32_spmd, body=%wide.region_28.31_spmd.sunk | while | flops 113705984 | bytes 25906324 | solution.py:71
  215.5 2.8 fusion.309
  234.6 9.2 %gather_fusion.1 = bf16[2048,512]{1,0:T(8,128)(2,1)} fusion(bf16[384,512]{1,0:T(8,128)(2,1)S(1)} %multiply_convert_fusion.1, s32[2048]{0:T(1024)S(1)} %broadcast_clamp_fusion), kind=kCustom, calls=%fused_computation.1 | custom fusion | bytes 4202496 | tf_op jit(solution)/shard_map/jit(_take)/gather | solution.py:95
  246.5 5.3 all-to-all-start
  253.1 28.8 %all-to-all-done = bf16[16,128,512]{2,1,0:T(8,128)(2,1)} async-done(((bf16[16,128,512]{2,1,0:T(8,128)(2,1)}), bf16[16,128,512]{2,1,0:T(8,128)(2,1)}, u32[]{:S(2)}, u32[]{:S(2)}) %all-to-all-start) | async-done | bytes 2097184 | tf_op jit(solution)/shard_map/all_to_all | solution.py:96
  284.5 3.8 convolution_convert_fusion
  288.2 5.7 all-to-all-start.1
  294.0 4.5 fusion.136
  298.4 25.5 %all-to-all-done.1 = bf16[16,128,512]{2,1,0:T(8,128)(2,1)} async-done(((bf16[16,128,512]{2,1,0:T(8,128)(2,1)}), bf16[16,128,512]{2,1,0:T(8,128)(2,1)}, u32[]{:S(2)}, u32[]{:S(2)}) %all-to-all-start.1) | async-done | bytes 2097184 | tf_op jit(solution)/shard_map/all_to_all | solution.py:134
  323.9 13.5 %scatter_custom_fusion = f32[384,512]{1,0:T(8,128)S(1)} fusion(s32[2048]{0:T(1024)} %bitcast.431, bf16[2048,512]{1,0:T(8,128)(2,1)} %bitcast.76, f32[]{:T(128)} %constant.623.clone.1), kind=kCustom, calls=%fused_computation.191 | custom fusion | flops 2097152 | bytes 2884096 | tf_op jit(solution)/shard_map/scatter-add | solution.py:142
  343.8 80.3 %all-reduce = (f32[]{:T(128)}, f32[]{:T(128)}) all-reduce(f32[]{:T(128)} %multiply_reduce_fusion.2, f32[]{:T(128)} %convert_reduce_fusion), channel_id=1, replica_groups=mesh['view'=2,'seq'=8,'event'=16] {'view','seq','event'}, use_global_device_ids=true, to_apply=%region_40.41 | all-reduce | flops 2 | bytes 16 | tf_op jit(solution)/shard_map/psum | solution.py:152
  425.5 175.0 %all-reduce.3.cloned.1.call-done = f32[512,512]{1,0:T(8,128)} async-done(((f32[512,512]{1,0:T(8,128)}), f32[512,512]{1,0:T(8,128)}) %all-reduce.3.cloned.1.call-update) | async-done | bytes 1048592 | tf_op jit(solution)/shard_map/psum | solution.py:152
  (397 shorter events, 200.8 us)
Async XLA Ops:
  7.2 226.8 %copy-start = (bf16[512,512]{1,0:T(8,128)(2,1)S(1)}, bf16[512,512]{1,0:T(8,128)(2,1)}, u32[]{:S(2)}) copy-start(bf16[512,512]{1,0:T(8,128)(2,1)} %param.29) | copy-start | bytes 1572868
  7.2 35.9 %collective-permute-start = (bf16[384,512]{1,0:T(8,128)(2,1)}, bf16[384,512]{1,0:T(8,128)(2,1)}, u32[]{:S(2)}, u32[]{:S(2)}) collective-permute-start(bf16[384,512]{1,0:T(8,128)(2,1)} %bitcast.423), channel_id=1, source_target_pairs={{0,16},{16,32},{32,48},{48,64},{64,80},{80,96},{96,112},{112,0},{1... | collective-permute-start | bytes 1179656 | tf_op jit(solution)/shard_map/ppermute | solution.py:14
  7.2 36.0 %collective-permute-start.1 = (bf16[384,512]{1,0:T(8,128)(2,1)}, bf16[384,512]{1,0:T(8,128)(2,1)}, u32[]{:S(2)}, u32[]{:S(2)}) collective-permute-start(bf16[384,512]{1,0:T(8,128)(2,1)} %bitcast.425), channel_id=1, source_target_pairs={{0,16},{16,32},{32,48},{48,64},{64,80},{80,96},{96,112},{112,0},{1... | collective-permute-start | bytes 1179656 | tf_op jit(solution)/shard_map/ppermute | solution.py:14
  11.1 31.9 %copy-start.8 = (s32[1,1,16,128]{3,2,1,0:T(8,128)S(1)}, s32[1,1,16,128]{3,2,1,0:T(8,128)}, u32[]{:S(2)}) copy-start(s32[1,1,16,128]{3,2,1,0:T(8,128)} %param.30) | copy-start | bytes 24580
  43.0 1.8 copy-start.9
  43.1 28.3 %collective-permute-start.2 = (bf16[384,512]{1,0:T(8,128)(2,1)}, bf16[384,512]{1,0:T(8,128)(2,1)}, u32[]{:S(2)}, u32[]{:S(2)}) collective-permute-start(bf16[384,512]{1,0:T(8,128)(2,1)} %collective-permute-done), channel_id=1, source_target_pairs={{0,16},{16,32},{32,48},{48,64},{64,80},{80,96},{96,112},{112,0},{1... | collective-permute-start | bytes 1179656 | tf_op jit(solution)/shard_map/ppermute | solution.py:14
  43.2 28.3 %collective-permute-start.3 = (bf16[384,512]{1,0:T(8,128)(2,1)}, bf16[384,512]{1,0:T(8,128)(2,1)}, u32[]{:S(2)}, u32[]{:S(2)}) collective-permute-start(bf16[384,512]{1,0:T(8,128)(2,1)} %collective-permute-done.1), channel_id=1, source_target_pairs={{0,16},{16,32},{32,48},{48,64},{64,80},{80,96},{96,112},{112,0},{1... | collective-permute-start | bytes 1179656 | tf_op jit(solution)/shard_map/ppermute | solution.py:14
  48.2 1.7 copy-start.1
  57.1 1.7 copy-start.1
  66.0 1.7 copy-start.1
  71.4 28.0 %collective-permute-start.4 = (bf16[384,512]{1,0:T(8,128)(2,1)}, bf16[384,512]{1,0:T(8,128)(2,1)}, u32[]{:S(2)}, u32[]{:S(2)}) collective-permute-start(bf16[384,512]{1,0:T(8,128)(2,1)} %collective-permute-done.2), channel_id=1, source_target_pairs={{0,16},{16,32},{32,48},{48,64},{64,80},{80,96},{96,112},{112,0},{1... | collective-permute-start | bytes 1179656 | tf_op jit(solution)/shard_map/ppermute | solution.py:14
  71.5 28.0 %collective-permute-start.5 = (bf16[384,512]{1,0:T(8,128)(2,1)}, bf16[384,512]{1,0:T(8,128)(2,1)}, u32[]{:S(2)}, u32[]{:S(2)}) collective-permute-start(bf16[384,512]{1,0:T(8,128)(2,1)} %collective-permute-done.3), channel_id=1, source_target_pairs={{0,16},{16,32},{32,48},{48,64},{64,80},{80,96},{96,112},{112,0},{1... | collective-permute-start | bytes 1179656 | tf_op jit(solution)/shard_map/ppermute | solution.py:14
  76.2 1.7 copy-start.2
  99.4 27.2 %collective-permute-start.6 = (bf16[384,512]{1,0:T(8,128)(2,1)}, bf16[384,512]{1,0:T(8,128)(2,1)}, u32[]{:S(2)}, u32[]{:S(2)}) collective-permute-start(bf16[384,512]{1,0:T(8,128)(2,1)} %collective-permute-done.4), channel_id=1, source_target_pairs={{0,16},{16,32},{32,48},{48,64},{64,80},{80,96},{96,112},{112,0},{1... | collective-permute-start | bytes 1179656 | tf_op jit(solution)/shard_map/ppermute | solution.py:14
  99.6 27.2 %collective-permute-start.7 = (bf16[384,512]{1,0:T(8,128)(2,1)}, bf16[384,512]{1,0:T(8,128)(2,1)}, u32[]{:S(2)}, u32[]{:S(2)}) collective-permute-start(bf16[384,512]{1,0:T(8,128)(2,1)} %collective-permute-done.5), channel_id=1, source_target_pairs={{0,16},{16,32},{32,48},{48,64},{64,80},{80,96},{96,112},{112,0},{1... | collective-permute-start | bytes 1179656 | tf_op jit(solution)/shard_map/ppermute | solution.py:14
  103.4 1.7 copy-start.3
  126.6 28.1 %collective-permute-start.8 = (bf16[384,512]{1,0:T(8,128)(2,1)}, bf16[384,512]{1,0:T(8,128)(2,1)}, u32[]{:S(2)}, u32[]{:S(2)}) collective-permute-start(bf16[384,512]{1,0:T(8,128)(2,1)} %collective-permute-done.6), channel_id=1, source_target_pairs={{0,16},{16,32},{32,48},{48,64},{64,80},{80,96},{96,112},{112,0},{1... | collective-permute-start | bytes 1179656 | tf_op jit(solution)/shard_map/ppermute | solution.py:14
  126.8 28.1 %collective-permute-start.9 = (bf16[384,512]{1,0:T(8,128)(2,1)}, bf16[384,512]{1,0:T(8,128)(2,1)}, u32[]{:S(2)}, u32[]{:S(2)}) collective-permute-start(bf16[384,512]{1,0:T(8,128)(2,1)} %collective-permute-done.7), channel_id=1, source_target_pairs={{0,16},{16,32},{32,48},{48,64},{64,80},{80,96},{96,112},{112,0},{1... | collective-permute-start | bytes 1179656 | tf_op jit(solution)/shard_map/ppermute | solution.py:14
  140.4 1.7 copy-start.4
  154.8 28.3 %collective-permute-start.10 = (bf16[384,512]{1,0:T(8,128)(2,1)}, bf16[384,512]{1,0:T(8,128)(2,1)}, u32[]{:S(2)}, u32[]{:S(2)}) collective-permute-start(bf16[384,512]{1,0:T(8,128)(2,1)} %collective-permute-done.8), channel_id=1, source_target_pairs={{0,16},{16,32},{32,48},{48,64},{64,80},{80,96},{96,112},{112,0},{1... | collective-permute-start | bytes 1179656 | tf_op jit(solution)/shard_map/ppermute | solution.py:14
  154.9 28.3 %collective-permute-start.11 = (bf16[384,512]{1,0:T(8,128)(2,1)}, bf16[384,512]{1,0:T(8,128)(2,1)}, u32[]{:S(2)}, u32[]{:S(2)}) collective-permute-start(bf16[384,512]{1,0:T(8,128)(2,1)} %collective-permute-done.9), channel_id=1, source_target_pairs={{0,16},{16,32},{32,48},{48,64},{64,80},{80,96},{96,112},{112,0},{1... | collective-permute-start | bytes 1179656 | tf_op jit(solution)/shard_map/ppermute | solution.py:14
  177.6 1.7 copy-start.5
  183.1 27.4 %collective-permute-start.12 = (bf16[384,512]{1,0:T(8,128)(2,1)}, bf16[384,512]{1,0:T(8,128)(2,1)S(1)}, u32[]{:S(2)}, u32[]{:S(2)}) collective-permute-start(bf16[384,512]{1,0:T(8,128)(2,1)} %collective-permute-done.10), channel_id=1, source_target_pairs={{0,16},{16,32},{32,48},{48,64},{64,80},{80,96},{96,112},{112,0},{1... | collective-permute-start | bytes 1179656 | tf_op jit(solution)/shard_map/ppermute | solution.py:14
  183.2 27.3 %collective-permute-start.13 = (bf16[384,512]{1,0:T(8,128)(2,1)}, bf16[384,512]{1,0:T(8,128)(2,1)S(1)}, u32[]{:S(2)}, u32[]{:S(2)}) collective-permute-start(bf16[384,512]{1,0:T(8,128)(2,1)} %collective-permute-done.11), channel_id=1, source_target_pairs={{0,16},{16,32},{32,48},{48,64},{64,80},{80,96},{96,112},{112,0},{1... | collective-permute-start | bytes 1179656 | tf_op jit(solution)/shard_map/ppermute | solution.py:14
  187.7 1.7 copy-start.6
  246.5 5.3 copy-start.11
  246.5 5.3 copy-start.10
  246.5 35.3 %copy-start.12 = (s32[1,1,256]{2,1,0:T(1,128)S(1)}, s32[1,1,256]{2,1,0:T(1,128)}, u32[]{:S(2)}) copy-start(s32[1,1,256]{2,1,0:T(1,128)} %param.32) | copy-start | bytes 3076
  246.5 35.3 %all-to-all-start = ((bf16[16,128,512]{2,1,0:T(8,128)(2,1)}), bf16[16,128,512]{2,1,0:T(8,128)(2,1)}, u32[]{:S(2)}, u32[]{:S(2)}) async-start(bf16[16,128,512]{2,1,0:T(8,128)(2,1)} %broadcast_select_fusion), calls=%async_computation | async-start | bytes 4194304 | tf_op jit(solution)/shard_map/all_to_all | solution.py:96
  284.5 3.8 copy-start.13
  288.2 35.7 %all-to-all-start.1 = ((bf16[16,128,512]{2,1,0:T(8,128)(2,1)}), bf16[16,128,512]{2,1,0:T(8,128)(2,1)}, u32[]{:S(2)}, u32[]{:S(2)}) async-start(bf16[16,128,512]{2,1,0:T(8,128)(2,1)} %bitcast.422), calls=%async_computation.1 | async-start | bytes 4194304 | tf_op jit(solution)/shard_map/all_to_all | solution.py:134
  293.9 306.5 %all-reduce.3.cloned.1.call-start = ((), (), s32[]{:S(2)}) async-start(), calls=%async_computation.2 | async-start | bytes 2097152 | tf_op jit(solution)/shard_map/psum | solution.py:152
  (13 other events, 21.7 us)
Sparse Core Ops, SparseCore 0:
  341.7 258.7 all-reduce.2
where the time goes:
time: 613 us; the launch traced here: 611 us
  waiting for transfers between devices  229 us (37%)
  matrix products  108 us (18%)
  local copies, waits for them, and re-layouts  91.3 us (15%)
  blocking collectives  80.3 us (13%)
  other arithmetic  62.2 us (10%)
  starting transfers between devices  21 us (3%)
  between operations  17 us (3%)
    psum x1, waiting for transfers between devices, per_device(): lax.psum((loss_term, loss_part, live_part), ('view', 'seq', 'event'))  175 us
    psum x1, blocking collectives, per_device(): lax.psum((loss_term, loss_part, live_part), ('view', 'seq', 'event'))  80.3 us
    dot_general x24, matrix products, one_group(): jnp.einsum('hqk,khd->hqd', weights.astype(jnp.bfloat16), head_values, pre...  67.5 us
    dynamic_slice x96, local copies, waits for them, and re-layouts, attend(): lax.scan(one_group, state, (key_groups, value_groups, offsets))  41.9 us
    while x66, local copies, waits for them, and re-layouts  34.6 us
    all_to_all x1, waiting for transfers between devices, per_device(): lax.all_to_all(outgoing, ('view', 'seq'), split_axis=0, concat_axis=0, ti...  28.8 us
    all_to_all x1, waiting for transfers between devices, per_device(): lax.all_to_all(candidate_grads.reshape(senders, capacity, width).astype(j...  25.5 us
    reduce_sum x24, other arithmetic, one_group(): total = total * factor + jnp.sum(weights, axis=-1)  24.6 us
  transfers between devices with their start and end apart: 17, of which 3 were waited for; matrix products, arithmetic and copies ran while one was open for 28% of the time, Pallas kernels for 0%

commit v1 on v0

--- a/solution.py
+++ b/solution.py
@@ -150,7 +150,7 @@
         mixed, embedding_gradients, (((0,), (0,)), ((), ())), preferred_element_type=jnp.float32
     )
     grad_total, loss_total, live_total = lax.psum(
-        (loss_term, loss_part, live_part), ("view", "seq", "event")
+        lax.psum((loss_term, loss_part, live_part), ("seq", "event")), "view"
     )
     return (mixed[None, None], grad_total, loss_total / live_total)
 

time: 613 us -> 1730 us (2.82)
  waiting for transfers between devices: 229 us -> 1130 us
  blocking collectives: 80.3 us -> 284 us
    psum x1 -> x2, waiting for transfers between devices: 175 us -> 1080 us  [the longest x1 1080 us: per_device(): lax.psum((loss_term, loss_part, live_part), ('seq', 'event'))]
    psum x1 -> x2, blocking collectives: 80.3 us -> 284 us  [the longest x1 277 us: per_device(): lax.psum((loss_term, loss_part, live_part), ('seq', 'event'))]
  transfers between devices with their start and end apart: 17 -> 18, of which waited for: 3 -> 3; matrix products, arithmetic and copies ran while one was open for 28% -> 10% of each run, Pallas kernels for 0% -> 0%
where the time goes in v1:
time: 1730 us; the launch traced here: 1720 us
  waiting for transfers between devices  1130 us (65%)
  blocking collectives  284 us (16%)
  matrix products  108 us (6%)
  local copies, waits for them, and re-layouts  92.1 us (5%)
  other arithmetic  63.2 us (4%)
  starting transfers between devices  20.9 us (1%)
    psum x1, waiting for transfers between devices, per_device(): lax.psum((loss_term, loss_part, live_part), ('seq', 'event'))  1080 us
    psum x1, blocking collectives, per_device(): lax.psum((loss_term, loss_part, live_part), ('seq', 'event'))  277 us
    dot_general x24, matrix products, one_group(): jnp.einsum('hqk,khd->hqd', weights.astype(jnp.bfloat16), head_values, pre...  67.5 us
    dynamic_slice x96, local copies, waits for them, and re-layouts, attend(): lax.scan(one_group, state, (key_groups, value_groups, offsets))  41.9 us
    while x66, local copies, waits for them, and re-layouts  34.6 us
  transfers between devices with their start and end apart: 18, of which 3 were waited for; matrix products, arithmetic and copies ran while one was open for 10% of the time, Pallas kernels for 0%

profile of v1, /device:TPU:2, one launch (start us, length us, event | category | flops | bytes accessed | tf_op | source)
XLA Modules:
  0.0 1719.3 jit_solution(8709646150008572913)
XLA Ops:
  11.1 31.8 %while.136 = (s32[]{:T(128)}, f32[16,384]{1,0:T(8,128)S(1)}, f32[16,384]{1,0:T(8,128)S(1)}, f32[16,384,32]{1,2,0:T(8,128)S(1)}, s32[3]{0:T(128)S(1)}, /*index=5*...) while((s32[]{:T(128)}, f32[16,384]{1,0:T(8,128)S(1)}, ...), condition=%wide.region_3.4_spmd.clone, body=%wide.region_0.3_spmd.clone.sunk | while | flops 113921024 | bytes 13323405 | solution.py:71
  18.8 2.8 fusion.319
  29.4 2.8 fusion.319
  40.0 2.8 fusion.319
  44.8 26.6 %while.129 = (s32[]{:T(128)}, f32[16,384]{1,0:T(8,128)S(1)}, f32[16,384]{1,0:T(8,128)S(1)}, f32[16,384,32]{1,2,0:T(8,128)S(1)}, s32[3]{0:T(128)S(1)}, /*index=5*...) while((s32[]{:T(128)}, f32[16,384]{1,0:T(8,128)S(1)}, ...), condition=%wide.region_7.8_spmd, body=%wide.region_4.7_spmd.sunk | while | flops 113705984 | bytes 25906324 | solution.py:71
  50.8 2.8 fusion.255
  59.7 2.8 fusion.255
  68.6 2.8 fusion.255
  72.8 26.6 %while.130 = (s32[]{:T(128)}, f32[16,384]{1,0:T(8,128)S(1)}, f32[16,384]{1,0:T(8,128)S(1)}, f32[16,384,32]{1,2,0:T(8,128)S(1)}, s32[3]{0:T(128)S(1)}, /*index=5*...) while((s32[]{:T(128)}, f32[16,384]{1,0:T(8,128)S(1)}, ...), condition=%wide.region_11.12_spmd, body=%wide.region_8.11_spmd.sunk | while | flops 113705984 | bytes 25906324 | solution.py:71
  78.8 2.8 fusion.264
  87.7 2.8 fusion.264
  100.0 26.6 %while.131 = (s32[]{:T(128)}, f32[16,384]{1,0:T(8,128)S(1)}, f32[16,384]{1,0:T(8,128)S(1)}, f32[16,384,32]{1,2,0:T(8,128)S(1)}, s32[3]{0:T(128)S(1)}, /*index=5*...) while((s32[]{:T(128)}, f32[16,384]{1,0:T(8,128)S(1)}, ...), condition=%wide.region_15.16_spmd, body=%wide.region_12.15_spmd.sunk | while | flops 113705984 | bytes 25906324 | solution.py:71
  114.9 2.8 fusion.273
  123.8 2.8 fusion.273
  128.1 26.6 %while.132 = (s32[]{:T(128)}, f32[16,384]{1,0:T(8,128)S(1)}, f32[16,384]{1,0:T(8,128)S(1)}, f32[16,384,32]{1,2,0:T(8,128)S(1)}, s32[3]{0:T(128)S(1)}, /*index=5*...) while((s32[]{:T(128)}, f32[16,384]{1,0:T(8,128)S(1)}, ...), condition=%wide.region_19.20_spmd, body=%wide.region_16.19_spmd.sunk | while | flops 113705984 | bytes 25906324 | solution.py:71
  134.2 2.8 fusion.282
  143.0 2.8 fusion.282
  156.5 26.6 %while.133 = (s32[]{:T(128)}, f32[16,384]{1,0:T(8,128)S(1)}, f32[16,384]{1,0:T(8,128)S(1)}, f32[16,384,32]{1,2,0:T(8,128)S(1)}, s32[3]{0:T(128)S(1)}, /*index=5*...) while((s32[]{:T(128)}, f32[16,384]{1,0:T(8,128)S(1)}, ...), condition=%wide.region_23.24_spmd, body=%wide.region_20.23_spmd.sunk | while | flops 113705984 | bytes 25906324 | solution.py:71
  162.5 2.8 fusion.291
  184.5 26.0 %while.134 = (s32[]{:T(128)}, f32[16,384]{1,0:T(8,128)S(1)}, f32[16,384]{1,0:T(8,128)S(1)}, f32[16,384,32]{1,2,0:T(8,128)S(1)}, s32[3]{0:T(128)S(1)}, /*index=5*...) while((s32[]{:T(128)}, f32[16,384]{1,0:T(8,128)S(1)}, ...), condition=%wide.region_27.28_spmd, body=%wide.region_24.27_spmd.sunk | while | flops 113705984 | bytes 25906324 | solution.py:71
  210.5 23.4 %while.135 = (s32[]{:T(128)}, f32[16,384]{1,0:T(8,128)S(1)}, f32[16,384]{1,0:T(8,128)S(1)}, f32[16,384,32]{1,2,0:T(8,128)S(1)}, s32[3]{0:T(128)S(1)}, /*index=5*...) while((s32[]{:T(128)}, f32[16,384]{1,0:T(8,128)S(1)}, ...), condition=%wide.region_31.32_spmd, body=%wide.region_28.31_spmd.sunk | while | flops 113705984 | bytes 25906324 | solution.py:71
  236.6 9.2 gather_fusion.1
  248.5 5.2 all-to-all-start
  254.9 28.8 %all-to-all-done = bf16[16,128,512]{2,1,0:T(8,128)(2,1)} async-done(((bf16[16,128,512]{2,1,0:T(8,128)(2,1)}), bf16[16,128,512]{2,1,0:T(8,128)(2,1)}, u32[]{:S(2)}, u32[]{:S(2)}) %all-to-all-start) | async-done | bytes 2097184 | tf_op jit(solution)/shard_map/all_to_all | solution.py:96
  286.3 3.8 convolution_convert_fusion
  290.1 5.7 all-to-all-start.1
  295.8 4.5 fusion.136
  300.3 25.5 %all-to-all-done.1 = bf16[16,128,512]{2,1,0:T(8,128)(2,1)} async-done(((bf16[16,128,512]{2,1,0:T(8,128)(2,1)}), bf16[16,128,512]{2,1,0:T(8,128)(2,1)}, u32[]{:S(2)}, u32[]{:S(2)}) %all-to-all-start.1) | async-done | bytes 2097184 | tf_op jit(solution)/shard_map/all_to_all | solution.py:134
  325.8 13.5 scatter_custom_fusion
  343.5 1078.2 %all-reduce.5.cloned.1.call-done = f32[512,512]{1,0:T(8,128)} async-done(((f32[512,512]{1,0:T(8,128)}), f32[512,512]{1,0:T(8,128)}) %all-reduce.5.cloned.1.call-update) | async-done | bytes 1048592 | tf_op jit(solution)/shard_map/psum | solution.py:153
  1423.9 276.8 %all-reduce = (f32[]{:T(128)}, f32[]{:T(128)}) all-reduce(f32[]{:T(128)} %multiply_reduce_fusion.2, f32[]{:T(128)} %convert_reduce_fusion), channel_id=1, replica_groups=mesh['view'=2,'seq'=8,'event'=16] {'seq','event'}, use_global_device_ids=true, to_apply=%region_41.42 | all-reduce | flops 2 | bytes 16 | tf_op jit(solution)/shard_map/psum | solution.py:153
  1700.7 7.1 all-reduce.1
  (403 shorter events, 205.6 us)
Async XLA Ops:
  7.2 228.8 %copy-start = (bf16[512,512]{1,0:T(8,128)(2,1)S(1)}, bf16[512,512]{1,0:T(8,128)(2,1)}, u32[]{:S(2)}) copy-start(bf16[512,512]{1,0:T(8,128)(2,1)} %param.29) | copy-start | bytes 1572868
  7.2 35.9 %collective-permute-start = (bf16[384,512]{1,0:T(8,128)(2,1)}, bf16[384,512]{1,0:T(8,128)(2,1)}, u32[]{:S(2)}, u32[]{:S(2)}) collective-permute-start(bf16[384,512]{1,0:T(8,128)(2,1)} %bitcast.423), channel_id=1, source_target_pairs={{0,16},{16,32},{32,48},{48,64},{64,80},{80,96},{96,112},{112,0},{1... | collective-permute-start | bytes 1179656 | tf_op jit(solution)/shard_map/ppermute | solution.py:14
  7.2 36.0 %collective-permute-start.1 = (bf16[384,512]{1,0:T(8,128)(2,1)}, bf16[384,512]{1,0:T(8,128)(2,1)}, u32[]{:S(2)}, u32[]{:S(2)}) collective-permute-start(bf16[384,512]{1,0:T(8,128)(2,1)} %bitcast.425), channel_id=1, source_target_pairs={{0,16},{16,32},{32,48},{48,64},{64,80},{80,96},{96,112},{112,0},{1... | collective-permute-start | bytes 1179656 | tf_op jit(solution)/shard_map/ppermute | solution.py:14
  11.1 31.9 %copy-start.9 = (s32[1,1,16,128]{3,2,1,0:T(8,128)S(1)}, s32[1,1,16,128]{3,2,1,0:T(8,128)}, u32[]{:S(2)}) copy-start(s32[1,1,16,128]{3,2,1,0:T(8,128)} %param.30) | copy-start | bytes 24580
  43.0 1.8 copy-start.10
  43.1 28.3 %collective-permute-start.2 = (bf16[384,512]{1,0:T(8,128)(2,1)}, bf16[384,512]{1,0:T(8,128)(2,1)}, u32[]{:S(2)}, u32[]{:S(2)}) collective-permute-start(bf16[384,512]{1,0:T(8,128)(2,1)} %collective-permute-done), channel_id=1, source_target_pairs={{0,16},{16,32},{32,48},{48,64},{64,80},{80,96},{96,112},{112,0},{1... | collective-permute-start | bytes 1179656 | tf_op jit(solution)/shard_map/ppermute | solution.py:14
  43.2 28.3 %collective-permute-start.3 = (bf16[384,512]{1,0:T(8,128)(2,1)}, bf16[384,512]{1,0:T(8,128)(2,1)}, u32[]{:S(2)}, u32[]{:S(2)}) collective-permute-start(bf16[384,512]{1,0:T(8,128)(2,1)} %collective-permute-done.1), channel_id=1, source_target_pairs={{0,16},{16,32},{32,48},{48,64},{64,80},{80,96},{96,112},{112,0},{1... | collective-permute-start | bytes 1179656 | tf_op jit(solution)/shard_map/ppermute | solution.py:14
  48.2 1.7 copy-start.1
  57.1 1.7 copy-start.1
  65.9 1.7 copy-start.1
  71.4 28.0 %collective-permute-start.4 = (bf16[384,512]{1,0:T(8,128)(2,1)}, bf16[384,512]{1,0:T(8,128)(2,1)}, u32[]{:S(2)}, u32[]{:S(2)}) collective-permute-start(bf16[384,512]{1,0:T(8,128)(2,1)} %collective-permute-done.2), channel_id=1, source_target_pairs={{0,16},{16,32},{32,48},{48,64},{64,80},{80,96},{96,112},{112,0},{1... | collective-permute-start | bytes 1179656 | tf_op jit(solution)/shard_map/ppermute | solution.py:14
  71.5 28.0 %collective-permute-start.5 = (bf16[384,512]{1,0:T(8,128)(2,1)}, bf16[384,512]{1,0:T(8,128)(2,1)}, u32[]{:S(2)}, u32[]{:S(2)}) collective-permute-start(bf16[384,512]{1,0:T(8,128)(2,1)} %collective-permute-done.3), channel_id=1, source_target_pairs={{0,16},{16,32},{32,48},{48,64},{64,80},{80,96},{96,112},{112,0},{1... | collective-permute-start | bytes 1179656 | tf_op jit(solution)/shard_map/ppermute | solution.py:14
  76.2 1.7 copy-start.2
  94.0 1.7 copy-start.2
  99.4 27.2 %collective-permute-start.6 = (bf16[384,512]{1,0:T(8,128)(2,1)}, bf16[384,512]{1,0:T(8,128)(2,1)}, u32[]{:S(2)}, u32[]{:S(2)}) collective-permute-start(bf16[384,512]{1,0:T(8,128)(2,1)} %collective-permute-done.4), channel_id=1, source_target_pairs={{0,16},{16,32},{32,48},{48,64},{64,80},{80,96},{96,112},{112,0},{1... | collective-permute-start | bytes 1179656 | tf_op jit(solution)/shard_map/ppermute | solution.py:14
  99.6 27.2 %collective-permute-start.7 = (bf16[384,512]{1,0:T(8,128)(2,1)}, bf16[384,512]{1,0:T(8,128)(2,1)}, u32[]{:S(2)}, u32[]{:S(2)}) collective-permute-start(bf16[384,512]{1,0:T(8,128)(2,1)} %collective-permute-done.5), channel_id=1, source_target_pairs={{0,16},{16,32},{32,48},{48,64},{64,80},{80,96},{96,112},{112,0},{1... | collective-permute-start | bytes 1179656 | tf_op jit(solution)/shard_map/ppermute | solution.py:14
  126.6 28.1 %collective-permute-start.8 = (bf16[384,512]{1,0:T(8,128)(2,1)}, bf16[384,512]{1,0:T(8,128)(2,1)}, u32[]{:S(2)}, u32[]{:S(2)}) collective-permute-start(bf16[384,512]{1,0:T(8,128)(2,1)} %collective-permute-done.6), channel_id=1, source_target_pairs={{0,16},{16,32},{32,48},{48,64},{64,80},{80,96},{96,112},{112,0},{1... | collective-permute-start | bytes 1179656 | tf_op jit(solution)/shard_map/ppermute | solution.py:14
  126.7 28.1 %collective-permute-start.9 = (bf16[384,512]{1,0:T(8,128)(2,1)}, bf16[384,512]{1,0:T(8,128)(2,1)}, u32[]{:S(2)}, u32[]{:S(2)}) collective-permute-start(bf16[384,512]{1,0:T(8,128)(2,1)} %collective-permute-done.7), channel_id=1, source_target_pairs={{0,16},{16,32},{32,48},{48,64},{64,80},{80,96},{96,112},{112,0},{1... | collective-permute-start | bytes 1179656 | tf_op jit(solution)/shard_map/ppermute | solution.py:14
  149.3 1.7 copy-start.4
  154.8 28.3 %collective-permute-start.10 = (bf16[384,512]{1,0:T(8,128)(2,1)}, bf16[384,512]{1,0:T(8,128)(2,1)}, u32[]{:S(2)}, u32[]{:S(2)}) collective-permute-start(bf16[384,512]{1,0:T(8,128)(2,1)} %collective-permute-done.8), channel_id=1, source_target_pairs={{0,16},{16,32},{32,48},{48,64},{64,80},{80,96},{96,112},{112,0},{1... | collective-permute-start | bytes 1179656 | tf_op jit(solution)/shard_map/ppermute | solution.py:14
  154.9 28.3 %collective-permute-start.11 = (bf16[384,512]{1,0:T(8,128)(2,1)}, bf16[384,512]{1,0:T(8,128)(2,1)}, u32[]{:S(2)}, u32[]{:S(2)}) collective-permute-start(bf16[384,512]{1,0:T(8,128)(2,1)} %collective-permute-done.9), channel_id=1, source_target_pairs={{0,16},{16,32},{32,48},{48,64},{64,80},{80,96},{96,112},{112,0},{1... | collective-permute-start | bytes 1179656 | tf_op jit(solution)/shard_map/ppermute | solution.py:14
  183.1 27.4 %collective-permute-start.12 = (bf16[384,512]{1,0:T(8,128)(2,1)}, bf16[384,512]{1,0:T(8,128)(2,1)S(1)}, u32[]{:S(2)}, u32[]{:S(2)}) collective-permute-start(bf16[384,512]{1,0:T(8,128)(2,1)} %collective-permute-done.10), channel_id=1, source_target_pairs={{0,16},{16,32},{32,48},{48,64},{64,80},{80,96},{96,112},{112,0},{1... | collective-permute-start | bytes 1179656 | tf_op jit(solution)/shard_map/ppermute | solution.py:14
  183.2 27.3 %collective-permute-start.13 = (bf16[384,512]{1,0:T(8,128)(2,1)}, bf16[384,512]{1,0:T(8,128)(2,1)S(1)}, u32[]{:S(2)}, u32[]{:S(2)}) collective-permute-start(bf16[384,512]{1,0:T(8,128)(2,1)} %collective-permute-done.11), channel_id=1, source_target_pairs={{0,16},{16,32},{32,48},{48,64},{64,80},{80,96},{96,112},{112,0},{1... | collective-permute-start | bytes 1179656 | tf_op jit(solution)/shard_map/ppermute | solution.py:14
  212.8 1.7 copy-start.7
  248.5 5.2 copy-start.12
  248.5 5.2 copy-start.11
  248.5 35.2 %copy-start.13 = (s32[1,1,256]{2,1,0:T(1,128)S(1)}, s32[1,1,256]{2,1,0:T(1,128)}, u32[]{:S(2)}) copy-start(s32[1,1,256]{2,1,0:T(1,128)} %param.32) | copy-start | bytes 3076
  248.5 35.2 %all-to-all-start = ((bf16[16,128,512]{2,1,0:T(8,128)(2,1)}), bf16[16,128,512]{2,1,0:T(8,128)(2,1)}, u32[]{:S(2)}, u32[]{:S(2)}) async-start(bf16[16,128,512]{2,1,0:T(8,128)(2,1)} %broadcast_select_fusion), calls=%async_computation | async-start | bytes 4194304 | tf_op jit(solution)/shard_map/all_to_all | solution.py:96
  286.3 3.8 copy-start.14
  290.1 35.7 %all-to-all-start.1 = ((bf16[16,128,512]{2,1,0:T(8,128)(2,1)}), bf16[16,128,512]{2,1,0:T(8,128)(2,1)}, u32[]{:S(2)}, u32[]{:S(2)}) async-start(bf16[16,128,512]{2,1,0:T(8,128)(2,1)} %bitcast.422), calls=%async_computation.1 | async-start | bytes 4194304 | tf_op jit(solution)/shard_map/all_to_all | solution.py:134
  295.8 1125.9 %all-reduce.5.cloned.1.call-start = ((), (), s32[]{:S(2)}) async-start(), calls=%async_computation.2 | async-start | bytes 2097152 | tf_op jit(solution)/shard_map/psum | solution.py:153
  343.4 1365.7 %all-reduce.7.cloned.1.call-start = ((), (), s32[]{:S(2)}) async-start(), calls=%async_computation.3 | async-start | bytes 2097152 | tf_op jit(solution)/shard_map/psum | solution.py:152
  (15 other events, 24.2 us)
Sparse Core Ops, SparseCore 0:
  343.5 1078.1 all-reduce.4
  1424.5 56.7 all-reduce.6
